TPU v7x, 32 devices: a whole 2x2x4 slice. The times are simulated.
32 devices in a mesh: space: 16 (over z, x, core), slab: 2 (over y).
Axes of the slice: x: 2, y: 2, z: 4, core: 2. Of those that a mesh axis runs over, the one named last changes fastest.
Arguments:
- charges: float32 [8192], P(('space', 'slab')), may hold values from -4 to 4
- fractions: float32 [3, 8192], P(None, ('space', 'slab')), may hold values from 0 to 1
- cell_x: int32 [8192], P(('space', 'slab')), may hold values from 0 to 15
- cell_y: int32 [8192], P(('space', 'slab')), may hold values from 0 to 7
- cell_z: int32 [8192], P(('space', 'slab')), may hold values from 0 to 127
- destination: int32 [8192, 1], P(('space', 'slab')), may hold values from 0 to 15; in each aligned block of 256 rows (0 to 255, 256 to 511, ...) at most 32 rows name the same one
Outputs:
- energy: float32 [8192], P(('space', 'slab'))
- forces: float32 [3, 8192], P(None, ('space', 'slab'))
Inputs may be any that keep to these rules, and one draw needn't show every extreme that they name: `destination`: among the atoms of one device no block is named by more than 32 atoms, and some block is named by exactly 32 of them.
All inputs are finite; a program needn't handle non-finite values.
Results may differ from a plain program's by a relative error of at most 0.0003.
Values sent between devices are 32-bit elements; how exact they have to be, the bound alone decides.
A program may use at most 128 MiB of HBM per device.

v0:
```python
import functools

import jax
import jax.numpy as jnp
import numpy as np
from jax import lax
from jax.experimental import pallas as pl
from jax.experimental.pallas import tpu as pltpu
from jax.sharding import PartitionSpec as P

CX = 16
NY = 8
CZ = 128
LANES = 128
WIDE = 2 * CZ
COULOMB = 332.0636 / 2.5
B0, B1, B2 = 0.75, 0.5, 0.125
OUT_X = CX + 3
REACH = 12
SIDE = REACH + 2
EXT_X = REACH + CX + REACH + 1
OUT_C = CX // 2 + 3
EXT_C = OUT_C + 8
FINE_S = sorted({a * a + b * b for a in range(5) for b in range(5)})
COARSE_S = sorted({a * a + b * b for a in range(5) for b in range(4)})
FULL_BELOW = 13
FINE_FULL = sum(s < FULL_BELOW for s in FINE_S)
COARSE_FULL = sum(s < FULL_BELOW for s in COARSE_S)
LEAD, TAIL = CZ + 16, 16
MESH = pl.DeviceIdType.MESH
F32 = jnp.float32
BF16 = jnp.bfloat16


def np_gamma(r):
    sq = r * r
    return np.where(r < 1.0, 1.875 - 1.25 * sq + 0.375 * sq * sq, 1.0 / np.maximum(r, 1.0))


def np_stencil(squares, level):
    r = np.sqrt(squares.astype(np.float64)) * 2.0**level
    c = 2.0 * 2.0**level
    return COULOMB * (np_gamma(r / c) / c - np_gamma(r / (2 * c)) / (2 * c))


def np_cells(count):
    lane = np.arange(count)
    return np.where(lane < 3 * count // 4, lane, lane - count)


def tables():
    def banded(cells, level, sums):
        lag = cells[:, None] - cells[None, :]
        parts = [np.where(abs(lag) <= 4, np_stencil(s + lag * lag, level), 0.0) for s in sums]
        return np.stack(parts).astype(np.float32)

    def split(t, full):
        high = t.astype(BF16)
        low = (t - high.astype(np.float32)).astype(BF16)
        return np.concatenate([high, low[:full]], axis=0)

    fine_cells, coarse_cells = np_cells(WIDE), np_cells(LANES)
    off = abs(fine_cells[:, None] - 2 * coarse_cells[None, :])
    rz = np.where(off == 0, B0, np.where(off == 1, B1, np.where(off == 2, B2, 0.0))).astype(BF16)
    fine = split(banded(fine_cells, 0, FINE_S), FINE_FULL)
    fine = np.concatenate([fine[:, :LEAD], fine[:, WIDE - TAIL :]], axis=1)
    return fine, split(banded(coarse_cells, 1, COARSE_S), COARSE_FULL), rz


def two(x):
    high = x.astype(BF16)
    return high, (x - high.astype(F32)).astype(BF16)


PLAIN = (((1,), (0,)), ((), ()))
TURNED = (((1,), (1,)), ((), ()))


def dot1(a, b, dims=PLAIN):
    return lax.dot_general(a, b, dims, preferred_element_type=F32)


def dot3(a, b, dims=PLAIN):
    return dot1(a[0], b[0], dims) + (dot1(a[0], b[1], dims) + dot1(a[1], b[0], dims))


def three_rows(x):
    high = x.astype(BF16).astype(F32)
    rest = x - high
    mid = rest.astype(BF16).astype(F32)
    return jnp.concatenate([high, mid, rest - mid], axis=0).astype(BF16)


def shift_y(x, step):
    if step == 0:
        return x
    rolled = pltpu.roll(x, (-step) % NY, 1)
    y = lax.broadcasted_iota(jnp.int32, x.shape, 1)
    keep = (y < NY - step) if step > 0 else (y >= -step)
    return jnp.where(keep, rolled, 0.0)


def pair_y(x, step):
    if step == 0:
        return x
    return shift_y(x, step) + shift_y(x, -step)


def rows2(x):
    return x.reshape(x.shape[0] * x.shape[1], x.shape[2])


def kernel(
    spaces, slabs, deltas, slot_size,
    charge_hbm, frac_hbm, x_hbm, y_hbm, z_hbm, dest_hbm, fine_hbm, coarse_hbm, rz_hbm,
    out_ref,
    charge_in, frac_in, x_in, y_in, z_in, dest_in, rz_ref, fine_tab, coarse_tab, place, send_buf, recv_buf, own_buf, left_buf, right_buf, res_buf, ret_buf,
    in_sem, tab_sem, self_sem, send_sem, recv_sem, halo_send, halo_recv, res_sem, ret_sem,
):
    i = lax.axis_index("space")
    l = lax.axis_index("slab")
    groups = len(deltas)
    atoms = charge_in.shape[1]
    slots = spaces * slot_size
    tiles = slots // LANES
    per_tile = LANES // slot_size

    def each(first):
        return pl.loop(first, spaces, unroll=spaces <= 16)

    def peer(k, g):
        return (lax.rem(i + k, spaces), lax.rem(l + deltas[g], slabs))

    barrier = pltpu.get_barrier_semaphore()
    for g in reversed(range(groups)):
        first = 1 if g == 0 else 0

        @each(first)
        def _(k):
            pl.semaphore_signal(barrier, inc=1, device_id=peer(k, g), device_id_type=MESH)

    arguments = (
        (charge_hbm, charge_in), (frac_hbm, frac_in), (x_hbm, x_in),
        (y_hbm, y_in), (z_hbm, z_in), (dest_hbm, dest_in),
    )
    arriving = [
        pltpu.make_async_copy(a, b, in_sem.at[n]) for n, (a, b) in enumerate(arguments)
    ]
    for copy in arriving:
        copy.start()
    fine_copy = pltpu.make_async_copy(
        fine_hbm.at[:, pl.ds(0, LEAD)], fine_tab.at[:, pl.ds(0, LEAD)], tab_sem.at[0]
    )
    fine_copy2 = pltpu.make_async_copy(
        fine_hbm.at[:, pl.ds(LEAD, TAIL)], fine_tab.at[:, pl.ds(WIDE - TAIL, TAIL)], tab_sem.at[3]
    )
    coarse_copy = pltpu.make_async_copy(coarse_hbm, coarse_tab, tab_sem.at[1])
    fine_copy.start()
    fine_copy2.start()
    coarse_copy.start()
    rz_copy = pltpu.make_async_copy(rz_hbm, rz_ref, tab_sem.at[2])
    rz_copy.start()

    @pl.when(i == 0)
    def _():
        left_buf[...] = jnp.zeros_like(left_buf)

    @pl.when(i == spaces - 1)
    def _():
        right_buf[...] = jnp.zeros_like(right_buf)

    for copy in arriving:
        copy.wait()
    dest = dest_in[...].astype(F32)
    payload = jnp.concatenate(
        [
            charge_in[...],
            frac_in[...],
            x_in[...].astype(F32),
            y_in[...].astype(F32),
            z_in[...].astype(F32),
            dest,
        ],
        axis=0,
    )
    chosen = (
        lax.broadcasted_iota(jnp.int32, (spaces, atoms), 0).astype(F32) == dest
    ).astype(F32)
    earlier = (
        lax.broadcasted_iota(jnp.int32, (atoms, atoms), 0)
        < lax.broadcasted_iota(jnp.int32, (atoms, atoms), 1)
    ).astype(F32).astype(BF16)
    counts = dot1(chosen.astype(BF16), earlier)
    rank = jnp.sum(chosen * counts, axis=0, keepdims=True)
    slot = dest * float(slot_size) + rank
    place[...] = (
        lax.broadcasted_iota(jnp.int32, (slots, atoms), 0).astype(F32) == slot
    ).astype(F32).astype(BF16)
    parts = dot1(three_rows(payload), place[...], TURNED)
    packed = parts[0:8] + parts[8:16] + parts[16:24]
    lane_part = lax.broadcasted_iota(jnp.int32, (8, LANES), 1) // slot_size
    row_part = lax.rem(lax.broadcasted_iota(jnp.int32, (8, LANES), 0), per_tile)
    columns = min(8, per_tile)

    def compact(value, count, out):
        for q in range(tiles):
            tile = value[:, q * LANES : (q + 1) * LANES]
            turned = [pltpu.roll(tile, n * slot_size, 1) if n else tile for n in range(per_tile)]
            for r in range(per_tile):
                merged = jnp.zeros((8, LANES), F32)
                for c in range(columns):
                    here = (lane_part == c) & (row_part == c)
                    merged = jnp.where(here, turned[(c - r) % per_tile], merged)
                for n in range(-(-count // per_tile)):
                    rows = merged[n * columns : (n + 1) * columns]
                    out[q * per_tile + r, n : n + 1] = jnp.sum(rows, axis=0, keepdims=True)

    compact(packed, 8, send_buf)

    fine_tab[:, LEAD : WIDE - TAIL] = jnp.zeros(
        (fine_tab.shape[0], WIDE - TAIL - LEAD, WIDE), BF16
    )
    pl.semaphore_wait(barrier, groups * spaces - 1)

    def atom_copy(k, g):
        target = peer(k, g)
        return pltpu.make_async_remote_copy(
            src_ref=send_buf.at[target[0]],
            dst_ref=recv_buf.at[g, i],
            send_sem=send_sem.at[g, k],
            recv_sem=recv_sem.at[g, i],
            device_id=target,
            device_id_type=MESH,
        )

    def atom_wait(k, g):
        source = lax.rem(i - k + spaces, spaces)
        return pltpu.make_async_remote_copy(
            src_ref=send_buf.at[0],
            dst_ref=recv_buf.at[g, source],
            send_sem=send_sem.at[g, k],
            recv_sem=recv_sem.at[g, source],
            device_id=peer(k, g),
            device_id_type=MESH,
        )

    for g in reversed(range(groups)):

        @each(1 if g == 0 else 0)
        def _(k):
            atom_copy(k, g).start()

    own_atoms = pltpu.make_async_copy(send_buf.at[i], recv_buf.at[0, i], self_sem.at[0])
    own_atoms.start()

    def regroup(piece_of):
        out = []
        for q in range(tiles):
            total = jnp.zeros((8, LANES), F32)
            for r in range(per_tile):
                piece = piece_of(q * per_tile + r)
                repeated = [
                    jnp.broadcast_to(piece[n : n + 1], (columns, LANES))
                    for n in range(piece.shape[0])
                ]
                while len(repeated) * columns < 8:
                    repeated.append(jnp.zeros((columns, LANES), F32))
                spread = jnp.concatenate(repeated, axis=0)
                for c in range(columns):
                    turn = (r - c) % per_tile * slot_size
                    turned = pltpu.roll(spread, turn, 1) if turn else spread
                    total = jnp.where((lane_part == r) & (row_part == c), turned, total)
            out.append(total)
        return jnp.concatenate(out, axis=1)

    def spline(t):
        u = 1.0 - t
        t2 = t * t
        t3 = t2 * t
        w = (
            u * u * u / 6.0,
            (3.0 * t3 - 6.0 * t2 + 4.0) / 6.0,
            (-3.0 * t3 + 3.0 * t2 + 3.0 * t + 1.0) / 6.0,
            t3 / 6.0,
        )
        s = (
            -u * u / 2.0,
            (3.0 * t2 - 4.0 * t) / 2.0,
            (-3.0 * t2 + 2.0 * t + 1.0) / 2.0,
            t2 / 2.0,
        )
        return w, s

    def spread_rows(weights, row, position):
        total = jnp.zeros(position.shape, F32)
        for k in range(4):
            total = jnp.where(position == float(k), weights[k][row : row + 1], total)
        return total

    row_x = lax.broadcasted_iota(jnp.int32, (24, slots), 0).astype(F32)
    row_y = lax.broadcasted_iota(jnp.int32, (NY, slots), 0).astype(F32) + 1.0

    own_rows = ((0, CZ + 16), (WIDE - 16, WIDE))
    side_rows = ((0, 16), (CZ - 16, CZ + 16), (WIDE - 16, WIDE))

    def z_matrix(weights, base, pieces):
        halves = ([], [])
        done = 0
        for first, end in pieces:
            if first > done:
                for h in halves:
                    h.append(jnp.zeros((first - done, slots), BF16))
            row = lax.broadcasted_iota(jnp.int32, (end - first, slots), 0) + first
            row = (row if end <= 3 * WIDE // 4 else row - WIDE).astype(F32) + 1.0
            for h, part in zip(halves, two(spread_rows(weights, 3, row - base))):
                h.append(part)
            done = end
        return tuple(jnp.concatenate(h, axis=0) for h in halves)

    for g in range(groups):

        @each(1 if g == 0 else 0)
        def _(k):
            atom_wait(k, g).wait_recv()

    own_atoms.wait()

    planes, zs = [], []
    for g in range(groups):
        got = regroup(lambda j: recv_buf[g, j])
        w, s = spline(got)
        mx = spread_rows(w, 1, row_x - got[4:5])
        my = spread_rows(w, 2, row_y - got[5:6])
        z_off = ((lax.rem(l - deltas[g] + slabs, slabs) - l) * CZ).astype(F32)
        z_base = got[6:7] + z_off
        mz = z_matrix(w, z_base, side_rows if g else own_rows)
        if g == 0:
            charge = got[0:1]
            own = (w, s, got, mx, my)
        cx = got[0:1] * mx
        plane = jnp.concatenate([cx[x : x + 1] * my for x in range(OUT_X)], axis=0)
        planes.append(two(plane))
        zs.append(mz)
    mz_split = zs[0]
    plane2 = [jnp.concatenate([p[h] for p in planes], axis=1) for h in range(2)]
    z2 = [jnp.concatenate([z[h] for z in zs], axis=1) for h in range(2)]
    own_buf[...] = dot3(plane2, z2, TURNED).reshape(OUT_X, NY, WIDE)

    right_copy = pltpu.make_async_remote_copy(
        src_ref=own_buf.at[pl.ds(OUT_X - SIDE, SIDE)], dst_ref=left_buf,
        send_sem=halo_send.at[0], recv_sem=halo_recv.at[0],
        device_id=(lax.rem(i + 1, spaces), l), device_id_type=MESH,
    )
    left_copy = pltpu.make_async_remote_copy(
        src_ref=own_buf.at[pl.ds(0, SIDE)], dst_ref=right_buf,
        send_sem=halo_send.at[1], recv_sem=halo_recv.at[1],
        device_id=(lax.rem(i + spaces - 1, spaces), l), device_id_type=MESH,
    )

    @pl.when(i < spaces - 1)
    def _():
        right_copy.start()

    @pl.when(i > 0)
    def _():
        left_copy.start()

    w, s, got, mx, my = own
    dx = spread_rows(s, 1, row_x - got[4:5])
    dy = spread_rows(s, 2, row_y - got[5:6])
    dz_split = z_matrix(s, got[6:7], own_rows)
    fine_copy.wait()
    fine_copy2.wait()
    coarse_copy.wait()
    rz_copy.wait()

    @pl.when(i > 0)
    def _():
        right_copy.wait_recv()

    @pl.when(i < spaces - 1)
    def _():
        left_copy.wait_recv()

    def inside(shape, first_x, block_x, block_z):
        ax = lax.broadcasted_iota(jnp.int32, shape, 0) + (i * block_x + first_x)
        az = lax.broadcasted_iota(jnp.int32, shape, 2)
        lanes = shape[2]
        az = jnp.where(az < 3 * lanes // 4, az, az - lanes) + l * block_z
        return (ax >= 0) & (ax < spaces * block_x) & (az >= 0) & (az < slabs * block_z)

    mid = own_buf[...]
    left = left_buf[...]
    right = right_buf[...]
    over = SIDE - REACH + 1
    grid = jnp.concatenate(
        [
            left[: SIDE - over],
            left[SIDE - over :] + mid[:over],
            mid[over : OUT_X - over],
            mid[OUT_X - over :] + right[:over],
            right[over:],
        ],
        axis=0,
    )
    grid = jnp.where(inside(grid.shape, -REACH, CX, CZ), grid, 0.0)

    def stencil(parts, table, kinds, full):
        depth = table.shape[1]
        high = table[:kinds].reshape(kinds * depth, table.shape[2])
        low = table[kinds:].reshape(full * depth, table.shape[2])
        a, b = parts
        near = full * depth
        return dot1(a, high) + (dot1(a[:, :near], low) + dot1(b, high[:near]))

    coarse = []
    for n in range(EXT_C):
        at = 2 * n + 2
        coarse.append(
            B0 * grid[at : at + 1]
            + B1 * (grid[at - 1 : at] + grid[at + 1 : at + 2])
            + B2 * (grid[at - 2 : at - 1] + grid[at + 2 : at + 3])
        )
    coarse = jnp.concatenate(coarse, axis=0)
    coarse = B0 * coarse + B1 * pair_y(coarse, 1) + B2 * pair_y(coarse, 2)
    high, low = two(rows2(coarse))
    rz = rz_ref[...]
    coarse = (dot1(high, rz) + dot1(low, rz)).reshape(EXT_C, NY, LANES)
    coarse = jnp.where(inside(coarse.shape, -5, CX // 2, CZ // 2), coarse, 0.0)

    def stack(source, out_count, step_y, reach_y, sums):
        shifted = [pair_y(source, step_y * d) if step_y * d < NY else None for d in range(reach_y)]
        highs, lows = [], []
        for square in sums:
            total = None
            for d in range(5):
                for e in range(reach_y):
                    if d * d + e * e != square:
                        continue
                    v = shifted[e]
                    term = v[4 + d : 4 + d + out_count]
                    if d:
                        term = term + v[4 - d : 4 - d + out_count]
                    total = term if total is None else total + term
            total = rows2(total)
            if square < FULL_BELOW:
                a, b = two(total)
                lows.append(b)
            else:
                a = total.astype(BF16)
            highs.append(a)
        return jnp.concatenate(highs, axis=1), jnp.concatenate(lows, axis=1)

    lifted = stencil(
        stack(coarse, OUT_C, 2, 4, COARSE_S), coarse_tab, len(COARSE_S), COARSE_FULL
    ).reshape(OUT_C, NY, LANES)
    even = lax.rem(lax.broadcasted_iota(jnp.int32, lifted.shape, 1), 2) == 0
    lifted = jnp.where(inside(lifted.shape, -1, CX // 2, CZ // 2) & even, lifted, 0.0)
    lifted = B0 * lifted + B1 * pair_y(lifted, 1) + B2 * pair_y(lifted, 2)
    high, low = two(rows2(lifted))
    lifted = (dot1(high, rz, TURNED) + dot1(low, rz, TURNED)).reshape(OUT_C, NY, WIDE)
    fine_lift = []
    for m in range(-1, CX + 2):
        n = m // 2 + 1
        if m % 2:
            fine_lift.append(B1 * (lifted[n : n + 1] + lifted[n + 1 : n + 2]))
        else:
            fine_lift.append(
                B0 * lifted[n : n + 1] + B2 * (lifted[n - 1 : n] + lifted[n + 1 : n + 2])
            )
    around = grid[REACH - 5 : REACH - 5 + OUT_X + 8]
    potential = stencil(
        stack(around, OUT_X, 1, 5, FINE_S), fine_tab, len(FINE_S), FINE_FULL
    ).reshape(OUT_X, NY, WIDE)
    potential = potential + jnp.concatenate(fine_lift, axis=0)
    potential = jnp.where(inside(potential.shape, -1, CX, CZ), potential, 0.0)

    pot = two(rows2(potential))
    through_w = dot3(pot, mz_split)
    through_d = dot3(pot, dz_split)
    along_w = along_dx = along_dz = jnp.zeros((NY, slots), F32)
    for x in range(OUT_X):
        tw = through_w[x * NY : (x + 1) * NY]
        td = through_d[x * NY : (x + 1) * NY]
        along_w = along_w + mx[x : x + 1] * tw
        along_dx = along_dx + dx[x : x + 1] * tw
        along_dz = along_dz + mx[x : x + 1] * td

    def down(v):
        return jnp.sum(v, axis=0, keepdims=True)

    results = jnp.concatenate(
        [
            0.5 * charge * down(my * along_w),
            -charge * down(my * along_dx),
            -charge * down(dy * along_w),
            -charge * down(my * along_dz),
            jnp.zeros((4, slots), F32),
        ],
        axis=0,
    )
    compact(results, 4, res_buf)

    def result_copy(k, source):
        target = lax.rem(i + k, spaces)
        return pltpu.make_async_remote_copy(
            src_ref=res_buf.at[target], dst_ref=ret_buf.at[source],
            send_sem=res_sem.at[k], recv_sem=ret_sem.at[source],
            device_id=(target, l), device_id_type=MESH,
        )

    @each(1)
    def _(k):
        result_copy(k, i).start()

    own_results = pltpu.make_async_copy(res_buf.at[i], ret_buf.at[i], self_sem.at[1])
    own_results.start()

    for g in range(groups):

        @each(1 if g == 0 else 0)
        def _(k):
            atom_wait(k, g).wait_send()

    @pl.when(i < spaces - 1)
    def _():
        right_copy.wait_send()

    @pl.when(i > 0)
    def _():
        left_copy.wait_send()

    @each(1)
    def _(k):
        result_copy(k, lax.rem(i - k + spaces, spaces)).wait_recv()

    own_results.wait()
    back = regroup(lambda j: ret_buf[j])
    parts = dot1(three_rows(back), place[...])
    final = parts[0:8] + parts[8:16] + parts[16:24]
    out_ref[...] = final

    @each(1)
    def _(k):
        result_copy(k, i).wait_send()


def per_device(spaces, slabs, charges, fractions, cell_x, cell_y, cell_z, destination):
    atoms = charges.shape[0]
    slot_size = 2 * atoms // spaces
    slots = spaces * slot_size
    deltas = (0,) if slabs == 1 else (0, 1) if slabs == 2 else (0, 1, slabs - 1)
    groups = len(deltas)
    fine, coarse, rz = tables()
    vmem = pl.BlockSpec(memory_space=pltpu.VMEM)
    atom_rows, result_rows = (-(-n * slot_size // LANES) for n in (8, 4))
    hbm = pl.BlockSpec(memory_space=pl.ANY)
    out = pl.pallas_call(
        functools.partial(kernel, spaces, slabs, deltas, slot_size),
        out_shape=pltpu.VMEM((8, atoms), F32),
        in_specs=[hbm] * 9,
        out_specs=vmem,
        scratch_shapes=[
            pltpu.VMEM((1, atoms), F32),
            pltpu.VMEM((3, atoms), F32),
            pltpu.VMEM((1, atoms), jnp.int32),
            pltpu.VMEM((1, atoms), jnp.int32),
            pltpu.VMEM((1, atoms), jnp.int32),
            pltpu.VMEM((1, atoms), jnp.int32),
            pltpu.VMEM(rz.shape, BF16),
            pltpu.VMEM((fine.shape[0], WIDE, WIDE), BF16),
            pltpu.VMEM(coarse.shape, BF16),
            pltpu.VMEM((slots, atoms), BF16),
            pltpu.VMEM((spaces, atom_rows, LANES), F32),
            pltpu.VMEM((groups, spaces, atom_rows, LANES), F32),
            pltpu.VMEM((OUT_X, NY, WIDE), F32),
            pltpu.VMEM((SIDE, NY, WIDE), F32),
            pltpu.VMEM((SIDE, NY, WIDE), F32),
            pltpu.VMEM((spaces, result_rows, LANES), F32),
            pltpu.VMEM((spaces, result_rows, LANES), F32),
            pltpu.SemaphoreType.DMA((6,)),
            pltpu.SemaphoreType.DMA((4,)),
            pltpu.SemaphoreType.DMA((2,)),
            pltpu.SemaphoreType.DMA((groups, spaces)),
            pltpu.SemaphoreType.DMA((groups, spaces)),
            pltpu.SemaphoreType.DMA((2,)),
            pltpu.SemaphoreType.DMA((2,)),
            pltpu.SemaphoreType.DMA((spaces,)),
            pltpu.SemaphoreType.DMA((spaces,)),
        ],
        compiler_params=pltpu.CompilerParams(collective_id=0, has_side_effects=True),
        name="multilevel",
    )(
        charges.reshape(1, atoms),
        fractions,
        cell_x.reshape(1, atoms),
        cell_y.reshape(1, atoms),
        cell_z.reshape(1, atoms),
        destination.reshape(1, atoms),
        jnp.asarray(fine),
        jnp.asarray(coarse),
        jnp.asarray(rz),
    )
    return out[0], out[1:4]


def solution(mesh):
    both = ("space", "slab")
    return jax.shard_map(
        functools.partial(per_device, mesh.shape["space"], mesh.shape["slab"]),
        mesh=mesh,
        in_specs=(P(both), P(None, both), P(both), P(both), P(both), P(both, None)),
        out_specs=(P(both), P(None, both)),
        check_vma=False,
    )
```

profile of v0, /device:TPU:0, one launch (start us, length us, event | category | flops | bytes accessed | tf_op | source)
XLA Modules:
  0.0 25.7 jit_solution(12673014092400805008)
XLA Ops:
  0.6 23.9 %multilevel.1 = f32[8,256]{1,0:T(8,128)S(1)} custom-call(f32[1,256]{1,0:T(1,128)} %bitcast.6, f32[3,256]{1,0:T(4,128)} %frac_hbm.1, s32[1,256]{1,0:T(1,128)} %bitcast.7, s32[1,256]{1,0:T(1,128)} %bitcast.8, s32[1,256]{1,0:T(1,128)} %bitcast.9, s32[1,256]{1,0:T(1,128)} %bitcast.10, bf16[23,160,256]{2,1,0:T(8,128)(2,1)} %constant.6.clone.fine_hbm, ...), custom_call_target="tpu_custom_call" | custom-call | tf_op jit(solution)/shard_map/multilevel/pallas_call | solution.py:558
  24.5 0.6 %slice.6 = f32[1,256]{1,0:T(1,128)} slice(f32[8,256]{1,0:T(8,128)S(1)} %multilevel.1), slice={[0:1], [0:256]} | slice | bytes 2048 | tf_op jit(solution)/shard_map/slice | solution.py:604
  25.1 0.6 %slice.7 = f32[3,256]{1,0:T(4,128)} slice(f32[8,256]{1,0:T(8,128)S(1)} %multilevel.1), slice={[1:4], [0:256]} | slice | bytes 6144 | tf_op jit(solution)/shard_map/slice | solution.py:604
where the time goes:
time: 25.8 us; the launch traced here: 25.7 us
  Pallas kernels  23.9 us (93%)
  local copies, waits for them, and re-layouts  1.16 us (4%)
  between operations  0.64 us (2%)
    pallas_call x1, Pallas kernels, per_device(): pl.pallas_call(functools.partial(kernel, spaces, slabs, deltas, slot_size...  23.9 us
    slice x2, local copies, waits for them, and re-layouts, per_device(): return (out[0], out[1:4])  1.16 us

commit v1 on v0

--- a/solution.py
+++ b/solution.py
@@ -114,8 +114,8 @@
     spaces, slabs, deltas, slot_size,
     charge_hbm, frac_hbm, x_hbm, y_hbm, z_hbm, dest_hbm, fine_hbm, coarse_hbm, rz_hbm,
     out_ref,
-    charge_in, frac_in, x_in, y_in, z_in, dest_in, rz_ref, fine_tab, coarse_tab, place, send_buf, recv_buf, own_buf, left_buf, right_buf, res_buf, ret_buf,
-    in_sem, tab_sem, self_sem, send_sem, recv_sem, halo_send, halo_recv, res_sem, ret_sem,
+    charge_in, frac_in, x_in, y_in, z_in, dest_in, rz_ref, fine_tab, coarse_tab, place, send_buf, stage_buf, relay_buf, recv_buf, own_buf, left_buf, right_buf, res_buf, ret_buf,
+    in_sem, tab_sem, self_sem, plane_send, plane_recv, send_sem, recv_sem, halo_send, halo_recv, res_sem, ret_sem,
 ):
     i = lax.axis_index("space")
     l = lax.axis_index("slab")
@@ -125,17 +125,26 @@
     tiles = slots // LANES
     per_tile = LANES // slot_size
 
-    def each(first):
-        return pl.loop(first, spaces, unroll=spaces <= 16)
+    block = per_tile
+    plane_of, in_plane = i // block, lax.rem(i, block)
+    width = block * LANES
+
+    def each(first, count=spaces):
+        return pl.loop(first, count, unroll=count <= 16)
+
+    def plane_peer(k):
+        return (lax.rem(plane_of + k, tiles) * block + in_plane, l)
 
     def peer(k, g):
-        return (lax.rem(i + k, spaces), lax.rem(l + deltas[g], slabs))
+        return (plane_of * block + lax.rem(in_plane + k, block), lax.rem(l + deltas[g], slabs))
 
     barrier = pltpu.get_barrier_semaphore()
+    for k in range(1, tiles):
+        pl.semaphore_signal(barrier, inc=1, device_id=plane_peer(k), device_id_type=MESH)
     for g in reversed(range(groups)):
         first = 1 if g == 0 else 0
 
-        @each(first)
+        @each(first, block)
         def _(k):
             pl.semaphore_signal(barrier, inc=1, device_id=peer(k, g), device_id_type=MESH)
 
@@ -203,40 +212,54 @@
     columns = min(8, per_tile)
 
     def compact(value, count, out):
-        for q in range(tiles):
+        for q in range(block):
             tile = value[:, q * LANES : (q + 1) * LANES]
             turned = [pltpu.roll(tile, n * slot_size, 1) if n else tile for n in range(per_tile)]
-            for r in range(per_tile):
+            for r in range(tiles):
                 merged = jnp.zeros((8, LANES), F32)
                 for c in range(columns):
                     here = (lane_part == c) & (row_part == c)
                     merged = jnp.where(here, turned[(c - r) % per_tile], merged)
                 for n in range(-(-count // per_tile)):
                     rows = merged[n * columns : (n + 1) * columns]
-                    out[q * per_tile + r, n : n + 1] = jnp.sum(rows, axis=0, keepdims=True)
-
-    compact(packed, 8, send_buf)
+                    out[r * block + q, n : n + 1] = jnp.sum(rows, axis=0, keepdims=True)
+
+    for q in range(tiles):
+        send_buf[q] = packed[:, q * LANES : (q + 1) * LANES]
 
     fine_tab[:, LEAD : WIDE - TAIL] = jnp.zeros(
         (fine_tab.shape[0], WIDE - TAIL - LEAD, WIDE), BF16
     )
-    pl.semaphore_wait(barrier, groups * spaces - 1)
-
-    def atom_copy(k, g):
-        target = peer(k, g)
+    pl.semaphore_wait(barrier, tiles - 1 + groups * block - 1)
+
+    def plane_copy(k, source):
+        target = plane_peer(k)
         return pltpu.make_async_remote_copy(
-            src_ref=send_buf.at[target[0]],
-            dst_ref=recv_buf.at[g, i],
-            send_sem=send_sem.at[g, k],
-            recv_sem=recv_sem.at[g, i],
+            src_ref=send_buf.at[lax.rem(plane_of + k, tiles)],
+            dst_ref=stage_buf.at[source],
+            send_sem=plane_send.at[k],
+            recv_sem=plane_recv.at[source],
             device_id=target,
             device_id_type=MESH,
         )
 
-    def atom_wait(k, g):
-        source = lax.rem(i - k + spaces, spaces)
+    for k in range(1, tiles):
+        plane_copy(k, plane_of).start()
+    stage_buf[plane_of] = send_buf[plane_of]
+    for k in range(1, tiles):
+        plane_copy(k, lax.rem(plane_of - k + tiles, tiles)).wait_recv()
+    staged = [stage_buf[q] for q in range(tiles)]
+    for n in range(block):
+        merged = jnp.zeros((8, LANES), F32)
+        for q in range(tiles):
+            turn = (q - n) * slot_size % LANES
+            turned = pltpu.roll(staged[q], turn, 1) if turn else staged[q]
+            merged = jnp.where(lane_part == q, turned, merged)
+        relay_buf[n] = merged
+
+    def atom_copy(k, g, source):
         return pltpu.make_async_remote_copy(
-            src_ref=send_buf.at[0],
+            src_ref=relay_buf.at[lax.rem(in_plane + k, block)],
             dst_ref=recv_buf.at[g, source],
             send_sem=send_sem.at[g, k],
             recv_sem=recv_sem.at[g, source],
@@ -246,12 +269,11 @@
 
     for g in reversed(range(groups)):
 
-        @each(1 if g == 0 else 0)
+        @each(1 if g == 0 else 0, block)
         def _(k):
-            atom_copy(k, g).start()
-
-    own_atoms = pltpu.make_async_copy(send_buf.at[i], recv_buf.at[0, i], self_sem.at[0])
-    own_atoms.start()
+            atom_copy(k, g, in_plane).start()
+
+    recv_buf[0, in_plane] = relay_buf[in_plane]
 
     def regroup(piece_of):
         out = []
@@ -297,8 +319,8 @@
             total = jnp.where(position == float(k), weights[k][row : row + 1], total)
         return total
 
-    row_x = lax.broadcasted_iota(jnp.int32, (24, slots), 0).astype(F32)
-    row_y = lax.broadcasted_iota(jnp.int32, (NY, slots), 0).astype(F32) + 1.0
+    row_x = lax.broadcasted_iota(jnp.int32, (24, width), 0).astype(F32)
+    row_y = lax.broadcasted_iota(jnp.int32, (NY, width), 0).astype(F32) + 1.0
 
     own_rows = ((0, CZ + 16), (WIDE - 16, WIDE))
     side_rows = ((0, 16), (CZ - 16, CZ + 16), (WIDE - 16, WIDE))
@@ -309,8 +331,8 @@
         for first, end in pieces:
             if first > done:
                 for h in halves:
-                    h.append(jnp.zeros((first - done, slots), BF16))
-            row = lax.broadcasted_iota(jnp.int32, (end - first, slots), 0) + first
+                    h.append(jnp.zeros((first - done, width), BF16))
+            row = lax.broadcasted_iota(jnp.int32, (end - first, width), 0) + first
             row = (row if end <= 3 * WIDE // 4 else row - WIDE).astype(F32) + 1.0
             for h, part in zip(halves, two(spread_rows(weights, 3, row - base))):
                 h.append(part)
@@ -319,15 +341,14 @@
 
     for g in range(groups):
 
-        @each(1 if g == 0 else 0)
+        @each(1 if g == 0 else 0, block)
         def _(k):
-            atom_wait(k, g).wait_recv()
-
-    own_atoms.wait()
+            atom_copy(k, g, lax.rem(in_plane - k + block, block)).wait_recv()
+
 
     planes, zs = [], []
     for g in range(groups):
-        got = regroup(lambda j: recv_buf[g, j])
+        got = jnp.concatenate([recv_buf[g, n] for n in range(block)], axis=1)
         w, s = spline(got)
         mx = spread_rows(w, 1, row_x - got[4:5])
         my = spread_rows(w, 2, row_y - got[5:6])
@@ -478,7 +499,7 @@
     pot = two(rows2(potential))
     through_w = dot3(pot, mz_split)
     through_d = dot3(pot, dz_split)
-    along_w = along_dx = along_dz = jnp.zeros((NY, slots), F32)
+    along_w = along_dx = along_dz = jnp.zeros((NY, width), F32)
     for x in range(OUT_X):
         tw = through_w[x * NY : (x + 1) * NY]
         td = through_d[x * NY : (x + 1) * NY]
@@ -495,7 +516,7 @@
             -charge * down(my * along_dx),
             -charge * down(dy * along_w),
             -charge * down(my * along_dz),
-            jnp.zeros((4, slots), F32),
+            jnp.zeros((4, width), F32),
         ],
         axis=0,
     )
@@ -513,14 +534,17 @@
     def _(k):
         result_copy(k, i).start()
 
-    own_results = pltpu.make_async_copy(res_buf.at[i], ret_buf.at[i], self_sem.at[1])
+    own_results = pltpu.make_async_copy(res_buf.at[i], ret_buf.at[i], self_sem.at[0])
     own_results.start()
 
     for g in range(groups):
 
-        @each(1 if g == 0 else 0)
+        @each(1 if g == 0 else 0, block)
         def _(k):
-            atom_wait(k, g).wait_send()
+            atom_copy(k, g, in_plane).wait_send()
+
+    for k in range(1, tiles):
+        plane_copy(k, plane_of).wait_send()
 
     @pl.when(i < spaces - 1)
     def _():
@@ -553,7 +577,8 @@
     groups = len(deltas)
     fine, coarse, rz = tables()
     vmem = pl.BlockSpec(memory_space=pltpu.VMEM)
-    atom_rows, result_rows = (-(-n * slot_size // LANES) for n in (8, 4))
+    result_rows = -(-4 * slot_size // LANES)
+    tiles, block = slots // LANES, LANES // slot_size
     hbm = pl.BlockSpec(memory_space=pl.ANY)
     out = pl.pallas_call(
         functools.partial(kernel, spaces, slabs, deltas, slot_size),
@@ -571,8 +596,10 @@
             pltpu.VMEM((fine.shape[0], WIDE, WIDE), BF16),
             pltpu.VMEM(coarse.shape, BF16),
             pltpu.VMEM((slots, atoms), BF16),
-            pltpu.VMEM((spaces, atom_rows, LANES), F32),
-            pltpu.VMEM((groups, spaces, atom_rows, LANES), F32),
+            pltpu.VMEM((tiles, 8, LANES), F32),
+            pltpu.VMEM((tiles, 8, LANES), F32),
+            pltpu.VMEM((block, 8, LANES), F32),
+            pltpu.VMEM((groups, block, 8, LANES), F32),
             pltpu.VMEM((OUT_X, NY, WIDE), F32),
             pltpu.VMEM((SIDE, NY, WIDE), F32),
             pltpu.VMEM((SIDE, NY, WIDE), F32),
@@ -580,9 +607,11 @@
             pltpu.VMEM((spaces, result_rows, LANES), F32),
             pltpu.SemaphoreType.DMA((6,)),
             pltpu.SemaphoreType.DMA((4,)),
-            pltpu.SemaphoreType.DMA((2,)),
-            pltpu.SemaphoreType.DMA((groups, spaces)),
-            pltpu.SemaphoreType.DMA((groups, spaces)),
+            pltpu.SemaphoreType.DMA((1,)),
+            pltpu.SemaphoreType.DMA((tiles,)),
+            pltpu.SemaphoreType.DMA((tiles,)),
+            pltpu.SemaphoreType.DMA((groups, block)),
+            pltpu.SemaphoreType.DMA((groups, block)),
             pltpu.SemaphoreType.DMA((2,)),
             pltpu.SemaphoreType.DMA((2,)),
             pltpu.SemaphoreType.DMA((spaces,)),

time: 25.8 us -> 27.1 us (1.050)
  Pallas kernels: 23.9 us -> 25.2 us
    pallas_call x1, Pallas kernels: 23.9 us -> 25.2 us  [per_device(): pl.pallas_call(functools.partial(kernel, spaces, slabs, deltas, slot_size...]
where the time goes in v1:
time: 27.1 us; the launch traced here: 27 us
  Pallas kernels  25.2 us (93%)
  local copies, waits for them, and re-layouts  1.16 us (4%)
  between operations  0.64 us (2%)
    pallas_call x1, Pallas kernels, per_device(): pl.pallas_call(functools.partial(kernel, spaces, slabs, deltas, slot_size...  25.2 us
    slice x2, local copies, waits for them, and re-layouts, per_device(): return (out[0], out[1:4])  1.16 us

profile of v1, /device:TPU:0, one launch (start us, length us, event | category | flops | bytes accessed | tf_op | source)
XLA Modules:
  0.0 27.0 jit_solution(1909081196284593866)
XLA Ops:
  0.6 25.2 %multilevel.1 = f32[8,256]{1,0:T(8,128)S(1)} custom-call(f32[1,256]{1,0:T(1,128)} %bitcast.6, f32[3,256]{1,0:T(4,128)} %frac_hbm.1, s32[1,256]{1,0:T(1,128)} %bitcast.7, s32[1,256]{1,0:T(1,128)} %bitcast.8, s32[1,256]{1,0:T(1,128)} %bitcast.9, s32[1,256]{1,0:T(1,128)} %bitcast.10, bf16[23,160,256]{2,1,0:T(8,128)(2,1)} %constant.6.clone.fine_hbm, ...), custom_call_target="tpu_custom_call" | custom-call | tf_op jit(solution)/shard_map/multilevel/pallas_call | solution.py:583
  25.8 0.6 %slice.6 = f32[1,256]{1,0:T(1,128)} slice(f32[8,256]{1,0:T(8,128)S(1)} %multilevel.1), slice={[0:1], [0:256]} | slice | bytes 2048 | tf_op jit(solution)/shard_map/slice | solution.py:633
  26.4 0.6 %slice.7 = f32[3,256]{1,0:T(4,128)} slice(f32[8,256]{1,0:T(8,128)S(1)} %multilevel.1), slice={[1:4], [0:256]} | slice | bytes 6144 | tf_op jit(solution)/shard_map/slice | solution.py:633

commit v2 on v0

--- a/solution.py
+++ b/solution.py
@@ -114,8 +114,8 @@
     spaces, slabs, deltas, slot_size,
     charge_hbm, frac_hbm, x_hbm, y_hbm, z_hbm, dest_hbm, fine_hbm, coarse_hbm, rz_hbm,
     out_ref,
-    charge_in, frac_in, x_in, y_in, z_in, dest_in, rz_ref, fine_tab, coarse_tab, place, send_buf, recv_buf, own_buf, left_buf, right_buf, res_buf, ret_buf,
-    in_sem, tab_sem, self_sem, send_sem, recv_sem, halo_send, halo_recv, res_sem, ret_sem,
+    charge_in, frac_in, x_in, y_in, z_in, dest_in, rz_ref, fine_tab, coarse_tab, place, send_buf, recv_buf, res_buf, ret_buf,
+    in_sem, tab_sem, self_sem, send_sem, recv_sem, res_sem, ret_sem,
 ):
     i = lax.axis_index("space")
     l = lax.axis_index("slab")
@@ -161,13 +161,8 @@
     rz_copy = pltpu.make_async_copy(rz_hbm, rz_ref, tab_sem.at[2])
     rz_copy.start()
 
-    @pl.when(i == 0)
-    def _():
-        left_buf[...] = jnp.zeros_like(left_buf)
-
-    @pl.when(i == spaces - 1)
-    def _():
-        right_buf[...] = jnp.zeros_like(right_buf)
+    for edge in (0, spaces + 1):
+        send_buf[edge] = jnp.zeros(send_buf.shape[1:], F32)
 
     for copy in arriving:
         copy.wait()
@@ -202,7 +197,7 @@
     row_part = lax.rem(lax.broadcasted_iota(jnp.int32, (8, LANES), 0), per_tile)
     columns = min(8, per_tile)
 
-    def compact(value, count, out):
+    def compact(value, count, out, skip=0):
         for q in range(tiles):
             tile = value[:, q * LANES : (q + 1) * LANES]
             turned = [pltpu.roll(tile, n * slot_size, 1) if n else tile for n in range(per_tile)]
@@ -213,9 +208,9 @@
                     merged = jnp.where(here, turned[(c - r) % per_tile], merged)
                 for n in range(-(-count // per_tile)):
                     rows = merged[n * columns : (n + 1) * columns]
-                    out[q * per_tile + r, n : n + 1] = jnp.sum(rows, axis=0, keepdims=True)
-
-    compact(packed, 8, send_buf)
+                    out[q * per_tile + r + skip, n : n + 1] = jnp.sum(rows, axis=0, keepdims=True)
+
+    compact(packed, 8, send_buf, 1)
 
     fine_tab[:, LEAD : WIDE - TAIL] = jnp.zeros(
         (fine_tab.shape[0], WIDE - TAIL - LEAD, WIDE), BF16
@@ -225,7 +220,7 @@
     def atom_copy(k, g):
         target = peer(k, g)
         return pltpu.make_async_remote_copy(
-            src_ref=send_buf.at[target[0]],
+            src_ref=send_buf.at[pl.ds(target[0], 3)],
             dst_ref=recv_buf.at[g, i],
             send_sem=send_sem.at[g, k],
             recv_sem=recv_sem.at[g, i],
@@ -236,7 +231,7 @@
     def atom_wait(k, g):
         source = lax.rem(i - k + spaces, spaces)
         return pltpu.make_async_remote_copy(
-            src_ref=send_buf.at[0],
+            src_ref=send_buf.at[pl.ds(0, 3)],
             dst_ref=recv_buf.at[g, source],
             send_sem=send_sem.at[g, k],
             recv_sem=recv_sem.at[g, source],
@@ -250,7 +245,7 @@
         def _(k):
             atom_copy(k, g).start()
 
-    own_atoms = pltpu.make_async_copy(send_buf.at[i], recv_buf.at[0, i], self_sem.at[0])
+    own_atoms = pltpu.make_async_copy(send_buf.at[pl.ds(i, 3)], recv_buf.at[0, i], self_sem.at[0])
     own_atoms.start()
 
     def regroup(piece_of):
@@ -325,47 +320,34 @@
 
     own_atoms.wait()
 
-    planes, zs = [], []
-    for g in range(groups):
-        got = regroup(lambda j: recv_buf[g, j])
-        w, s = spline(got)
-        mx = spread_rows(w, 1, row_x - got[4:5])
-        my = spread_rows(w, 2, row_y - got[5:6])
-        z_off = ((lax.rem(l - deltas[g] + slabs, slabs) - l) * CZ).astype(F32)
-        z_base = got[6:7] + z_off
-        mz = z_matrix(w, z_base, side_rows if g else own_rows)
-        if g == 0:
-            charge = got[0:1]
-            own = (w, s, got, mx, my)
-        cx = got[0:1] * mx
-        plane = jnp.concatenate([cx[x : x + 1] * my for x in range(OUT_X)], axis=0)
-        planes.append(two(plane))
-        zs.append(mz)
-    mz_split = zs[0]
-    plane2 = [jnp.concatenate([p[h] for p in planes], axis=1) for h in range(2)]
-    z2 = [jnp.concatenate([z[h] for z in zs], axis=1) for h in range(2)]
-    own_buf[...] = dot3(plane2, z2, TURNED).reshape(OUT_X, NY, WIDE)
-
-    right_copy = pltpu.make_async_remote_copy(
-        src_ref=own_buf.at[pl.ds(OUT_X - SIDE, SIDE)], dst_ref=left_buf,
-        send_sem=halo_send.at[0], recv_sem=halo_recv.at[0],
-        device_id=(lax.rem(i + 1, spaces), l), device_id_type=MESH,
-    )
-    left_copy = pltpu.make_async_remote_copy(
-        src_ref=own_buf.at[pl.ds(0, SIDE)], dst_ref=right_buf,
-        send_sem=halo_send.at[1], recv_sem=halo_recv.at[1],
-        device_id=(lax.rem(i + spaces - 1, spaces), l), device_id_type=MESH,
-    )
-
-    @pl.when(i < spaces - 1)
-    def _():
-        right_copy.start()
-
-    @pl.when(i > 0)
-    def _():
-        left_copy.start()
-
-    w, s, got, mx, my = own
+    def spread(part, first_row, rows):
+        planes, zs, kept = [], [], None
+        for g in range(groups):
+            got = regroup(lambda j: recv_buf[g, j, part])
+            w, s = spline(got)
+            mx = spread_rows(w, 1, row_x - got[4:5])
+            my = spread_rows(w, 2, row_y - got[5:6])
+            z_off = ((lax.rem(l - deltas[g] + slabs, slabs) - l) * CZ).astype(F32)
+            z_base = got[6:7] + z_off
+            mz = z_matrix(w, z_base, side_rows if g else own_rows)
+            if g == 0:
+                kept = (w, s, got, mx, my, mz)
+            cx = got[0:1] * mx
+            plane = jnp.concatenate(
+                [cx[x : x + 1] * my for x in range(first_row, first_row + rows)], axis=0
+            )
+            planes.append(two(plane))
+            zs.append(mz)
+        plane2 = [jnp.concatenate([p[h] for p in planes], axis=1) for h in range(2)]
+        z2 = [jnp.concatenate([z[h] for z in zs], axis=1) for h in range(2)]
+        return dot3(plane2, z2, TURNED).reshape(rows, NY, WIDE), kept
+
+    mid, own = spread(1, 0, OUT_X)
+    left, _ = spread(0, OUT_X - SIDE, SIDE)
+    right, _ = spread(2, 0, SIDE)
+
+    w, s, got, mx, my, mz_split = own
+    charge = got[0:1]
     dx = spread_rows(s, 1, row_x - got[4:5])
     dy = spread_rows(s, 2, row_y - got[5:6])
     dz_split = z_matrix(s, got[6:7], own_rows)
@@ -374,14 +356,6 @@
     coarse_copy.wait()
     rz_copy.wait()
 
-    @pl.when(i > 0)
-    def _():
-        right_copy.wait_recv()
-
-    @pl.when(i < spaces - 1)
-    def _():
-        left_copy.wait_recv()
-
     def inside(shape, first_x, block_x, block_z):
         ax = lax.broadcasted_iota(jnp.int32, shape, 0) + (i * block_x + first_x)
         az = lax.broadcasted_iota(jnp.int32, shape, 2)
@@ -389,9 +363,6 @@
         az = jnp.where(az < 3 * lanes // 4, az, az - lanes) + l * block_z
         return (ax >= 0) & (ax < spaces * block_x) & (az >= 0) & (az < slabs * block_z)
 
-    mid = own_buf[...]
-    left = left_buf[...]
-    right = right_buf[...]
     over = SIDE - REACH + 1
     grid = jnp.concatenate(
         [
@@ -521,14 +492,6 @@
         @each(1 if g == 0 else 0)
         def _(k):
             atom_wait(k, g).wait_send()
-
-    @pl.when(i < spaces - 1)
-    def _():
-        right_copy.wait_send()
-
-    @pl.when(i > 0)
-    def _():
-        left_copy.wait_send()
 
     @each(1)
     def _(k):
@@ -571,11 +534,8 @@
             pltpu.VMEM((fine.shape[0], WIDE, WIDE), BF16),
             pltpu.VMEM(coarse.shape, BF16),
             pltpu.VMEM((slots, atoms), BF16),
-            pltpu.VMEM((spaces, atom_rows, LANES), F32),
-            pltpu.VMEM((groups, spaces, atom_rows, LANES), F32),
-            pltpu.VMEM((OUT_X, NY, WIDE), F32),
-            pltpu.VMEM((SIDE, NY, WIDE), F32),
-            pltpu.VMEM((SIDE, NY, WIDE), F32),
+            pltpu.VMEM((spaces + 2, atom_rows, LANES), F32),
+            pltpu.VMEM((groups, spaces, 3, atom_rows, LANES), F32),
             pltpu.VMEM((spaces, result_rows, LANES), F32),
             pltpu.VMEM((spaces, result_rows, LANES), F32),
             pltpu.SemaphoreType.DMA((6,)),
@@ -583,8 +543,6 @@
             pltpu.SemaphoreType.DMA((2,)),
             pltpu.SemaphoreType.DMA((groups, spaces)),
             pltpu.SemaphoreType.DMA((groups, spaces)),
-            pltpu.SemaphoreType.DMA((2,)),
-            pltpu.SemaphoreType.DMA((2,)),
             pltpu.SemaphoreType.DMA((spaces,)),
             pltpu.SemaphoreType.DMA((spaces,)),
         ],

time: 25.8 us -> 24.8 us (0.961)
  Pallas kernels: 23.9 us -> 22.8 us
    pallas_call x1, Pallas kernels: 23.9 us -> 22.8 us  [per_device(): pl.pallas_call(functools.partial(kernel, spaces, slabs, deltas, slot_size...]
where the time goes in v2:
time: 24.8 us; the launch traced here: 24.6 us
  Pallas kernels  22.8 us (92%)
  local copies, waits for them, and re-layouts  1.16 us (5%)
  between operations  0.64 us (3%)
    pallas_call x1, Pallas kernels, per_device(): pl.pallas_call(functools.partial(kernel, spaces, slabs, deltas, slot_size...  22.8 us
    slice x2, local copies, waits for them, and re-layouts, per_device(): return (out[0], out[1:4])  1.16 us

profile of v2, /device:TPU:0, one launch (start us, length us, event | category | flops | bytes accessed | tf_op | source)
XLA Modules:
  0.0 24.6 jit_solution(4782587617661986438)
XLA Ops:
  0.6 22.8 %multilevel.1 = f32[8,256]{1,0:T(8,128)S(1)} custom-call(f32[1,256]{1,0:T(1,128)} %bitcast.6, f32[3,256]{1,0:T(4,128)} %frac_hbm.1, s32[1,256]{1,0:T(1,128)} %bitcast.7, s32[1,256]{1,0:T(1,128)} %bitcast.8, s32[1,256]{1,0:T(1,128)} %bitcast.9, s32[1,256]{1,0:T(1,128)} %bitcast.10, bf16[23,160,256]{2,1,0:T(8,128)(2,1)} %constant.6.clone.fine_hbm, ...), custom_call_target="tpu_custom_call" | custom-call | tf_op jit(solution)/shard_map/multilevel/pallas_call | solution.py:521
  23.4 0.6 %slice.6 = f32[1,256]{1,0:T(1,128)} slice(f32[8,256]{1,0:T(8,128)S(1)} %multilevel.1), slice={[0:1], [0:256]} | slice | bytes 2048 | tf_op jit(solution)/shard_map/slice | solution.py:562
  24.0 0.6 %slice.7 = f32[3,256]{1,0:T(4,128)} slice(f32[8,256]{1,0:T(8,128)S(1)} %multilevel.1), slice={[1:4], [0:256]} | slice | bytes 6144 | tf_op jit(solution)/shard_map/slice | solution.py:562

commit v3 on v2

--- a/solution.py
+++ b/solution.py
@@ -57,7 +57,7 @@
     def split(t, full):
         high = t.astype(BF16)
         low = (t - high.astype(np.float32)).astype(BF16)
-        return np.concatenate([high, low[:full]], axis=0)
+        return np.concatenate([high[:full], -high[full:], -low[:full]], axis=0)
 
     fine_cells, coarse_cells = np_cells(WIDE), np_cells(LANES)
     off = abs(fine_cells[:, None] - 2 * coarse_cells[None, :])
@@ -80,8 +80,14 @@
     return lax.dot_general(a, b, dims, preferred_element_type=F32)
 
 
-def dot3(a, b, dims=PLAIN):
-    return dot1(a[0], b[0], dims) + (dot1(a[0], b[1], dims) + dot1(a[1], b[0], dims))
+def two_rows(x):
+    high = x.astype(BF16).astype(F32)
+    return jnp.concatenate([high, x - high], axis=0).astype(BF16)
+
+
+def dot3(rows, both, b, dims=PLAIN):
+    wide = dot1(both, b[0], dims)
+    return wide[:rows] + wide[rows:] - dot1(both[:rows], b[1], dims)
 
 
 def three_rows(x):
@@ -299,16 +305,30 @@
     side_rows = ((0, 16), (CZ - 16, CZ + 16), (WIDE - 16, WIDE))
 
     def z_matrix(weights, base, pieces):
+        def packed_rows(v):
+            return jnp.broadcast_to(v, (16, slots)).astype(BF16)
+
+        base = packed_rows(base - 1.0)
+        highs = [weights[k][3:4].astype(BF16).astype(F32) for k in range(4)]
+        lows = [packed_rows(highs[k] - weights[k][3:4]) for k in range(4)]
+        highs = [packed_rows(v) for v in highs]
+        low_row = lax.broadcasted_iota(jnp.int32, (16, slots), 0).astype(F32)
         halves = ([], [])
         done = 0
         for first, end in pieces:
             if first > done:
                 for h in halves:
                     h.append(jnp.zeros((first - done, slots), BF16))
-            row = lax.broadcasted_iota(jnp.int32, (end - first, slots), 0) + first
-            row = (row if end <= 3 * WIDE // 4 else row - WIDE).astype(F32) + 1.0
-            for h, part in zip(halves, two(spread_rows(weights, 3, row - base))):
-                h.append(part)
+            shift = 0 if end <= 3 * WIDE // 4 else WIDE
+            for row in range(first - shift, end - shift, 16):
+                lag = (low_row + float(row)).astype(BF16) - base
+                high = low = jnp.zeros((16, slots), BF16)
+                for k in range(4):
+                    here = lag == jnp.array(k, BF16)
+                    high = jnp.where(here, highs[k], high)
+                    low = jnp.where(here, lows[k], low)
+                halves[0].append(high)
+                halves[1].append(low)
             done = end
         return tuple(jnp.concatenate(h, axis=0) for h in halves)
 
@@ -336,11 +356,11 @@
             plane = jnp.concatenate(
                 [cx[x : x + 1] * my for x in range(first_row, first_row + rows)], axis=0
             )
-            planes.append(two(plane))
+            planes.append(two_rows(plane))
             zs.append(mz)
-        plane2 = [jnp.concatenate([p[h] for p in planes], axis=1) for h in range(2)]
+        plane2 = jnp.concatenate(planes, axis=1)
         z2 = [jnp.concatenate([z[h] for z in zs], axis=1) for h in range(2)]
-        return dot3(plane2, z2, TURNED).reshape(rows, NY, WIDE), kept
+        return dot3(rows * NY, plane2, z2, TURNED).reshape(rows, NY, WIDE), kept
 
     mid, own = spread(1, 0, OUT_X)
     left, _ = spread(0, OUT_X - SIDE, SIDE)
@@ -376,13 +396,15 @@
     )
     grid = jnp.where(inside(grid.shape, -REACH, CX, CZ), grid, 0.0)
 
-    def stencil(parts, table, kinds, full):
-        depth = table.shape[1]
-        high = table[:kinds].reshape(kinds * depth, table.shape[2])
-        low = table[kinds:].reshape(full * depth, table.shape[2])
-        a, b = parts
-        near = full * depth
-        return dot1(a, high) + (dot1(a[:, :near], low) + dot1(b, high[:near]))
+    def stencil(parts, table, full):
+        near, far = parts
+        rows, depth = far.shape[0], table.shape[1]
+        wide = dot1(near, table[:full].reshape(full * depth, table.shape[2]))
+        rest = dot1(
+            jnp.concatenate([far, near[:rows]], axis=1),
+            table[full:].reshape(-1, table.shape[2]),
+        )
+        return wide[:rows] + wide[rows:] - rest
 
     coarse = []
     for n in range(EXT_C):
@@ -401,7 +423,7 @@
 
     def stack(source, out_count, step_y, reach_y, sums):
         shifted = [pair_y(source, step_y * d) if step_y * d < NY else None for d in range(reach_y)]
-        highs, lows = [], []
+        near, far = [], []
         for square in sums:
             total = None
             for d in range(5):
@@ -415,15 +437,13 @@
                     total = term if total is None else total + term
             total = rows2(total)
             if square < FULL_BELOW:
-                a, b = two(total)
-                lows.append(b)
+                near.append(two_rows(total))
             else:
-                a = total.astype(BF16)
-            highs.append(a)
-        return jnp.concatenate(highs, axis=1), jnp.concatenate(lows, axis=1)
+                far.append(total.astype(BF16))
+        return jnp.concatenate(near, axis=1), jnp.concatenate(far, axis=1)
 
     lifted = stencil(
-        stack(coarse, OUT_C, 2, 4, COARSE_S), coarse_tab, len(COARSE_S), COARSE_FULL
+        stack(coarse, OUT_C, 2, 4, COARSE_S), coarse_tab, COARSE_FULL
     ).reshape(OUT_C, NY, LANES)
     even = lax.rem(lax.broadcasted_iota(jnp.int32, lifted.shape, 1), 2) == 0
     lifted = jnp.where(inside(lifted.shape, -1, CX // 2, CZ // 2) & even, lifted, 0.0)
@@ -441,14 +461,14 @@
             )
     around = grid[REACH - 5 : REACH - 5 + OUT_X + 8]
     potential = stencil(
-        stack(around, OUT_X, 1, 5, FINE_S), fine_tab, len(FINE_S), FINE_FULL
+        stack(around, OUT_X, 1, 5, FINE_S), fine_tab, FINE_FULL
     ).reshape(OUT_X, NY, WIDE)
     potential = potential + jnp.concatenate(fine_lift, axis=0)
     potential = jnp.where(inside(potential.shape, -1, CX, CZ), potential, 0.0)
 
-    pot = two(rows2(potential))
-    through_w = dot3(pot, mz_split)
-    through_d = dot3(pot, dz_split)
+    pot = two_rows(rows2(potential))
+    through_w = dot3(OUT_X * NY, pot, mz_split)
+    through_d = dot3(OUT_X * NY, pot, dz_split)
     along_w = along_dx = along_dz = jnp.zeros((NY, slots), F32)
     for x in range(OUT_X):
         tw = through_w[x * NY : (x + 1) * NY]

time: 24.8 us -> 22.6 us (0.911)
  Pallas kernels: 22.8 us -> 20.6 us
    pallas_call x1, Pallas kernels: 22.8 us -> 20.6 us  [per_device(): pl.pallas_call(functools.partial(kernel, spaces, slabs, deltas, slot_size...]
where the time goes in v3:
time: 22.6 us; the launch traced here: 22.4 us
  Pallas kernels  20.6 us (91%)
  local copies, waits for them, and re-layouts  1.16 us (5%)
  between operations  0.64 us (3%)
    pallas_call x1, Pallas kernels, per_device(): pl.pallas_call(functools.partial(kernel, spaces, slabs, deltas, slot_size...  20.6 us
    slice x2, local copies, waits for them, and re-layouts, per_device(): return (out[0], out[1:4])  1.16 us

profile of v3, /device:TPU:0, one launch (start us, length us, event | category | flops | bytes accessed | tf_op | source)
XLA Modules:
  0.0 22.4 jit_solution(599637580781469526)
XLA Ops:
  0.6 20.6 %multilevel.1 = f32[8,256]{1,0:T(8,128)S(1)} custom-call(f32[1,256]{1,0:T(1,128)} %bitcast.6, f32[3,256]{1,0:T(4,128)} %frac_hbm.1, s32[1,256]{1,0:T(1,128)} %bitcast.7, s32[1,256]{1,0:T(1,128)} %bitcast.8, s32[1,256]{1,0:T(1,128)} %bitcast.9, s32[1,256]{1,0:T(1,128)} %bitcast.10, bf16[23,160,256]{2,1,0:T(8,128)(2,1)} %constant.6.clone.fine_hbm, ...), custom_call_target="tpu_custom_call" | custom-call | tf_op jit(solution)/shard_map/multilevel/pallas_call | solution.py:541
  21.2 0.6 %slice.6 = f32[1,256]{1,0:T(1,128)} slice(f32[8,256]{1,0:T(8,128)S(1)} %multilevel.1), slice={[0:1], [0:256]} | slice | bytes 2048 | tf_op jit(solution)/shard_map/slice | solution.py:582
  21.8 0.6 %slice.7 = f32[3,256]{1,0:T(4,128)} slice(f32[8,256]{1,0:T(8,128)S(1)} %multilevel.1), slice={[1:4], [0:256]} | slice | bytes 6144 | tf_op jit(solution)/shard_map/slice | solution.py:582

commit v4 on v3

--- a/solution.py
+++ b/solution.py
@@ -121,7 +121,7 @@
     charge_hbm, frac_hbm, x_hbm, y_hbm, z_hbm, dest_hbm, fine_hbm, coarse_hbm, rz_hbm,
     out_ref,
     charge_in, frac_in, x_in, y_in, z_in, dest_in, rz_ref, fine_tab, coarse_tab, place, send_buf, recv_buf, res_buf, ret_buf,
-    in_sem, tab_sem, self_sem, send_sem, recv_sem, res_sem, ret_sem,
+    in_sem, tab_sem, send_sem, recv_sem, res_sem, ret_sem,
 ):
     i = lax.axis_index("space")
     l = lax.axis_index("slab")
@@ -150,21 +150,21 @@
         (y_hbm, y_in), (z_hbm, z_in), (dest_hbm, dest_in),
     )
     arriving = [
-        pltpu.make_async_copy(a, b, in_sem.at[n]) for n, (a, b) in enumerate(arguments)
+        pltpu.make_async_copy(a, b, in_sem) for a, b in arguments
     ]
     for copy in arriving:
         copy.start()
     fine_copy = pltpu.make_async_copy(
-        fine_hbm.at[:, pl.ds(0, LEAD)], fine_tab.at[:, pl.ds(0, LEAD)], tab_sem.at[0]
+        fine_hbm.at[:, pl.ds(0, LEAD)], fine_tab.at[:, pl.ds(0, LEAD)], tab_sem
     )
     fine_copy2 = pltpu.make_async_copy(
-        fine_hbm.at[:, pl.ds(LEAD, TAIL)], fine_tab.at[:, pl.ds(WIDE - TAIL, TAIL)], tab_sem.at[3]
-    )
-    coarse_copy = pltpu.make_async_copy(coarse_hbm, coarse_tab, tab_sem.at[1])
+        fine_hbm.at[:, pl.ds(LEAD, TAIL)], fine_tab.at[:, pl.ds(WIDE - TAIL, TAIL)], tab_sem
+    )
+    coarse_copy = pltpu.make_async_copy(coarse_hbm, coarse_tab, tab_sem)
     fine_copy.start()
     fine_copy2.start()
     coarse_copy.start()
-    rz_copy = pltpu.make_async_copy(rz_hbm, rz_ref, tab_sem.at[2])
+    rz_copy = pltpu.make_async_copy(rz_hbm, rz_ref, tab_sem)
     rz_copy.start()
 
     for edge in (0, spaces + 1):
@@ -228,22 +228,14 @@
         return pltpu.make_async_remote_copy(
             src_ref=send_buf.at[pl.ds(target[0], 3)],
             dst_ref=recv_buf.at[g, i],
-            send_sem=send_sem.at[g, k],
-            recv_sem=recv_sem.at[g, i],
+            send_sem=send_sem,
+            recv_sem=recv_sem,
             device_id=target,
             device_id_type=MESH,
         )
 
-    def atom_wait(k, g):
-        source = lax.rem(i - k + spaces, spaces)
-        return pltpu.make_async_remote_copy(
-            src_ref=send_buf.at[pl.ds(0, 3)],
-            dst_ref=recv_buf.at[g, source],
-            send_sem=send_sem.at[g, k],
-            recv_sem=recv_sem.at[g, source],
-            device_id=peer(k, g),
-            device_id_type=MESH,
-        )
+    def arrived(ref, sem):
+        return pltpu.make_async_copy(ref, ref, sem)
 
     for g in reversed(range(groups)):
 
@@ -251,7 +243,7 @@
         def _(k):
             atom_copy(k, g).start()
 
-    own_atoms = pltpu.make_async_copy(send_buf.at[pl.ds(i, 3)], recv_buf.at[0, i], self_sem.at[0])
+    own_atoms = pltpu.make_async_copy(send_buf.at[pl.ds(i, 3)], recv_buf.at[0, i], recv_sem)
     own_atoms.start()
 
     def regroup(piece_of):
@@ -332,13 +324,11 @@
             done = end
         return tuple(jnp.concatenate(h, axis=0) for h in halves)
 
-    for g in range(groups):
-
-        @each(1 if g == 0 else 0)
-        def _(k):
-            atom_wait(k, g).wait_recv()
-
-    own_atoms.wait()
+    fine_copy.wait()
+    fine_copy2.wait()
+    coarse_copy.wait()
+    rz_copy.wait()
+    arrived(recv_buf, recv_sem).wait()
 
     def spread(part, first_row, rows):
         planes, zs, kept = [], [], None
@@ -371,10 +361,6 @@
     dx = spread_rows(s, 1, row_x - got[4:5])
     dy = spread_rows(s, 2, row_y - got[5:6])
     dz_split = z_matrix(s, got[6:7], own_rows)
-    fine_copy.wait()
-    fine_copy2.wait()
-    coarse_copy.wait()
-    rz_copy.wait()
 
     def inside(shape, first_x, block_x, block_z):
         ax = lax.broadcasted_iota(jnp.int32, shape, 0) + (i * block_x + first_x)
@@ -492,40 +478,32 @@
     )
     compact(results, 4, res_buf)
 
-    def result_copy(k, source):
+    def result_copy(k):
         target = lax.rem(i + k, spaces)
         return pltpu.make_async_remote_copy(
-            src_ref=res_buf.at[target], dst_ref=ret_buf.at[source],
-            send_sem=res_sem.at[k], recv_sem=ret_sem.at[source],
+            src_ref=res_buf.at[target], dst_ref=ret_buf.at[i],
+            send_sem=res_sem, recv_sem=ret_sem,
             device_id=(target, l), device_id_type=MESH,
         )
 
     @each(1)
     def _(k):
-        result_copy(k, i).start()
-
-    own_results = pltpu.make_async_copy(res_buf.at[i], ret_buf.at[i], self_sem.at[1])
+        result_copy(k).start()
+
+    own_results = pltpu.make_async_copy(res_buf.at[i], ret_buf.at[i], ret_sem)
     own_results.start()
 
     for g in range(groups):
-
-        @each(1 if g == 0 else 0)
-        def _(k):
-            atom_wait(k, g).wait_send()
-
-    @each(1)
-    def _(k):
-        result_copy(k, lax.rem(i - k + spaces, spaces)).wait_recv()
-
-    own_results.wait()
+        sent = recv_buf.at[g] if g else recv_buf.at[0, pl.ds(1, spaces - 1)]
+        arrived(sent, send_sem).wait()
+
+    arrived(ret_buf, ret_sem).wait()
     back = regroup(lambda j: ret_buf[j])
     parts = dot1(three_rows(back), place[...])
     final = parts[0:8] + parts[8:16] + parts[16:24]
     out_ref[...] = final
 
-    @each(1)
-    def _(k):
-        result_copy(k, i).wait_send()
+    arrived(ret_buf.at[pl.ds(1, spaces - 1)], res_sem).wait()
 
 
 def per_device(spaces, slabs, charges, fractions, cell_x, cell_y, cell_z, destination):
@@ -558,13 +536,7 @@
             pltpu.VMEM((groups, spaces, 3, atom_rows, LANES), F32),
             pltpu.VMEM((spaces, result_rows, LANES), F32),
             pltpu.VMEM((spaces, result_rows, LANES), F32),
-            pltpu.SemaphoreType.DMA((6,)),
-            pltpu.SemaphoreType.DMA((4,)),
-            pltpu.SemaphoreType.DMA((2,)),
-            pltpu.SemaphoreType.DMA((groups, spaces)),
-            pltpu.SemaphoreType.DMA((groups, spaces)),
-            pltpu.SemaphoreType.DMA((spaces,)),
-            pltpu.SemaphoreType.DMA((spaces,)),
+            *[pltpu.SemaphoreType.DMA(()) for _ in range(6)],
         ],
         compiler_params=pltpu.CompilerParams(collective_id=0, has_side_effects=True),
         name="multilevel",

time: 22.6 us -> 21.4 us (0.947)
  Pallas kernels: 20.6 us -> 19.4 us
    pallas_call x1, Pallas kernels: 20.6 us -> 19.4 us  [per_device(): pl.pallas_call(functools.partial(kernel, spaces, slabs, deltas, slot_size...]
where the time goes in v4:
time: 21.4 us; the launch traced here: 21.2 us
  Pallas kernels  19.4 us (91%)
  local copies, waits for them, and re-layouts  1.16 us (5%)
  between operations  0.64 us (3%)
    pallas_call x1, Pallas kernels, per_device(): pl.pallas_call(functools.partial(kernel, spaces, slabs, deltas, slot_size...  19.4 us
    slice x2, local copies, waits for them, and re-layouts, per_device(): return (out[0], out[1:4])  1.16 us

profile of v4, /device:TPU:0, one launch (start us, length us, event | category | flops | bytes accessed | tf_op | source)
XLA Modules:
  0.0 21.2 jit_solution(3747041352333427810)
XLA Ops:
  0.6 19.4 %multilevel.1 = f32[8,256]{1,0:T(8,128)S(1)} custom-call(f32[1,256]{1,0:T(1,128)} %bitcast.6, f32[3,256]{1,0:T(4,128)} %frac_hbm.1, s32[1,256]{1,0:T(1,128)} %bitcast.7, s32[1,256]{1,0:T(1,128)} %bitcast.8, s32[1,256]{1,0:T(1,128)} %bitcast.9, s32[1,256]{1,0:T(1,128)} %bitcast.10, bf16[23,160,256]{2,1,0:T(8,128)(2,1)} %constant.6.clone.fine_hbm, ...), custom_call_target="tpu_custom_call" | custom-call | tf_op jit(solution)/shard_map/multilevel/pallas_call | solution.py:519
  20.0 0.6 %slice.6 = f32[1,256]{1,0:T(1,128)} slice(f32[8,256]{1,0:T(8,128)S(1)} %multilevel.1), slice={[0:1], [0:256]} | slice | bytes 2048 | tf_op jit(solution)/shard_map/slice | solution.py:554
  20.6 0.6 %slice.7 = f32[3,256]{1,0:T(4,128)} slice(f32[8,256]{1,0:T(8,128)S(1)} %multilevel.1), slice={[1:4], [0:256]} | slice | bytes 6144 | tf_op jit(solution)/shard_map/slice | solution.py:554

commit v5 on v4

--- a/solution.py
+++ b/solution.py
@@ -138,12 +138,13 @@
         return (lax.rem(i + k, spaces), lax.rem(l + deltas[g], slabs))
 
     barrier = pltpu.get_barrier_semaphore()
-    for g in reversed(range(groups)):
-        first = 1 if g == 0 else 0
-
-        @each(first)
-        def _(k):
+    @each(1)
+    def _(k):
+        for g in reversed(range(groups)):
             pl.semaphore_signal(barrier, inc=1, device_id=peer(k, g), device_id_type=MESH)
+
+    for g in range(1, groups):
+        pl.semaphore_signal(barrier, inc=1, device_id=peer(0, g), device_id_type=MESH)
 
     arguments = (
         (charge_hbm, charge_in), (frac_hbm, frac_in), (x_hbm, x_in),
@@ -224,7 +225,7 @@
     pl.semaphore_wait(barrier, groups * spaces - 1)
 
     def atom_copy(k, g):
-        target = peer(k, g)
+        target = peer(spaces - k, g)
         return pltpu.make_async_remote_copy(
             src_ref=send_buf.at[pl.ds(target[0], 3)],
             dst_ref=recv_buf.at[g, i],
@@ -237,11 +238,13 @@
     def arrived(ref, sem):
         return pltpu.make_async_copy(ref, ref, sem)
 
-    for g in reversed(range(groups)):
-
-        @each(1 if g == 0 else 0)
-        def _(k):
+    @each(1)
+    def _(k):
+        for g in reversed(range(groups)):
             atom_copy(k, g).start()
+
+    for g in range(1, groups):
+        atom_copy(0, g).start()
 
     own_atoms = pltpu.make_async_copy(send_buf.at[pl.ds(i, 3)], recv_buf.at[0, i], recv_sem)
     own_atoms.start()

time: 21.4 us -> 20.6 us (0.963)
  Pallas kernels: 19.4 us -> 18.7 us
    pallas_call x1, Pallas kernels: 19.4 us -> 18.7 us  [per_device(): pl.pallas_call(functools.partial(kernel, spaces, slabs, deltas, slot_size...]
where the time goes in v5:
time: 20.6 us; the launch traced here: 20.5 us
  Pallas kernels  18.7 us (91%)
  local copies, waits for them, and re-layouts  1.16 us (6%)
  between operations  0.64 us (3%)
    pallas_call x1, Pallas kernels, per_device(): pl.pallas_call(functools.partial(kernel, spaces, slabs, deltas, slot_size...  18.7 us
    slice x2, local copies, waits for them, and re-layouts, per_device(): return (out[0], out[1:4])  1.16 us

profile of v5, /device:TPU:0, one launch (start us, length us, event | category | flops | bytes accessed | tf_op | source)
XLA Modules:
  0.0 20.5 jit_solution(5731687434998446503)
XLA Ops:
  0.6 18.7 %multilevel.1 = f32[8,256]{1,0:T(8,128)S(1)} custom-call(f32[1,256]{1,0:T(1,128)} %bitcast.6, f32[3,256]{1,0:T(4,128)} %frac_hbm.1, s32[1,256]{1,0:T(1,128)} %bitcast.7, s32[1,256]{1,0:T(1,128)} %bitcast.8, s32[1,256]{1,0:T(1,128)} %bitcast.9, s32[1,256]{1,0:T(1,128)} %bitcast.10, bf16[23,160,256]{2,1,0:T(8,128)(2,1)} %constant.6.clone.fine_hbm, ...), custom_call_target="tpu_custom_call" | custom-call | tf_op jit(solution)/shard_map/multilevel/pallas_call | solution.py:522
  19.3 0.6 %slice.6 = f32[1,256]{1,0:T(1,128)} slice(f32[8,256]{1,0:T(8,128)S(1)} %multilevel.1), slice={[0:1], [0:256]} | slice | bytes 2048 | tf_op jit(solution)/shard_map/slice | solution.py:557
  19.9 0.6 %slice.7 = f32[3,256]{1,0:T(4,128)} slice(f32[8,256]{1,0:T(8,128)S(1)} %multilevel.1), slice={[1:4], [0:256]} | slice | bytes 6144 | tf_op jit(solution)/shard_map/slice | solution.py:557
